TPU v7x, 256 devices: a whole 4x4x8 slice. The times are simulated.
256 devices in a mesh: seq: 64 (over x, z, core), ch: 4 (over y).
Axes of the slice: x: 4, y: 4, z: 8, core: 2. Of those that a mesh axis runs over, the one named last changes fastest.
Arguments:
- proj: bfloat16 [3, 128, 65536], P(None, 'ch', 'seq'), may hold values from -6 to 6
- cotangent: bfloat16 [128, 65536], P('ch', 'seq'), may hold values from -6 to 6
- short_w: float32 [3, 128, 3], P(None, 'ch'), may hold values from -3.5 to 3.5
- filter_in: float32 [32, 64], replicated, may hold values from -5 to 5
- filter_out: float32 [64, 128], P(None, 'ch'), may hold values from -0.75 to 0.75
- rates: float32 [128], P('ch'), may hold values from 0.25 to 2184
Outputs:
- grad_proj: bfloat16 [3, 128, 65536], P(None, 'ch', 'seq')
- grad_short: float32 [3, 128, 3], P(None, 'ch')
- grad_filter_out: float32 [64, 128], P(None, 'ch')
- grad_filter_in: float32 [32, 64], replicated
All inputs are finite; a program needn't handle non-finite values.
Results may differ from a plain program's by a relative error of at most 0.0013.
Values may be sent and summed in bfloat16 or wider, within the bound.
A program may use at most 64 MiB of HBM per device.

v0:
```python
import math
import jax
import jax.numpy as jnp
from jax import lax
from jax.sharding import PartitionSpec as P

PRECISE = lax.Precision.HIGHEST


def shifted(value, axis, by):
    length = lax.axis_size(axis)
    pairs = [(i, i + by) for i in range(length) if 0 <= i + by < length]
    return lax.ppermute(value, axis, pairs)


def position_features(positions, length, feature_count):
    feature_index = jnp.arange(feature_count, dtype=jnp.int32)
    multiplier = (1 + feature_index // 2 * 499) % length
    upper = positions // 1024
    lower = positions % 1024
    phases = (
        upper[:, None] * (multiplier * 1024 % length)[None, :]
        + lower[:, None] * multiplier[None, :]
    ) % length
    angles = phases.astype(jnp.float32) * (2.0 * math.pi / length)
    return jnp.where((feature_index % 2 == 0)[None, :], jnp.cos(angles), jnp.sin(angles))


def angle_tables(row_count, col_count, row_start, col_start, modulus):
    row_index = row_start + jnp.arange(row_count, dtype=jnp.int32)
    col_index = col_start + jnp.arange(col_count, dtype=jnp.int32)
    phases = row_index[:, None] * col_index[None, :] % modulus
    angles = phases.astype(jnp.float32) * (2.0 * math.pi / modulus)
    return (jnp.cos(angles), jnp.sin(angles))


def rotate(real_part, imag_part, cosine, sine, sign):
    return (
        real_part * cosine - sign * imag_part * sine,
        imag_part * cosine + sign * real_part * sine,
    )


def dft_axis(real_part, imag_part, form, cosine, sine, sign):
    real_cos = jnp.einsum(form, real_part, cosine, precision=PRECISE)
    real_sin = jnp.einsum(form, real_part, sine, precision=PRECISE)
    imag_cos = jnp.einsum(form, imag_part, cosine, precision=PRECISE)
    imag_sin = jnp.einsum(form, imag_part, sine, precision=PRECISE)
    return (real_cos - sign * imag_sin, imag_cos + sign * real_sin)


def shards(proj, cotangent, short_w, filter_in, filter_out, rates):
    tap_count = short_w.shape[2]
    channels = proj.shape[1]
    devices = lax.axis_size("seq")
    tokens_here = proj.shape[2]
    length = devices * tokens_here
    modulus = 2 * length
    norm_scale = 1.0 / math.sqrt(length)
    column_width = tokens_here // devices
    first_split = math.gcd(tokens_here, 64)
    second_split = tokens_here // first_split
    device_index = lax.axis_index("seq")
    rim_cols = shifted(proj[:, :, tokens_here - (tap_count - 1) :], "seq", 1)
    extended = jnp.concatenate([rim_cols, proj], 2).astype(jnp.float32)

    def delayed(offset):
        return extended[:, :, tap_count - 1 - offset : tap_count - 1 - offset + tokens_here]

    mixed_all = short_w[:, :, 0, None] * delayed(0)
    for offset in range(1, tap_count):
        mixed_all = mixed_all + short_w[:, :, offset, None] * delayed(offset)
    query_part, key_part, value_part = (mixed_all[0], mixed_all[1], mixed_all[2])
    gated_prod = key_part * value_part
    cotangent_full = cotangent.astype(jnp.float32)
    grad_conv = cotangent_full * query_part
    both_signals = jnp.concatenate([gated_prod, grad_conv], 0).reshape(2 * channels, 1, tokens_here)
    columns = lax.all_to_all(both_signals, "seq", split_axis=2, concat_axis=1, tiled=True)
    block_start = jnp.arange(devices, dtype=jnp.int32) * tokens_here
    offset_start = device_index * column_width + jnp.arange(column_width, dtype=jnp.int32)
    column_pos = (block_start[:, None] + offset_start[None, :]).reshape(devices * column_width)
    features = position_features(column_pos, length, filter_in.shape[0])
    preact = jnp.dot(features, filter_in, precision=PRECISE, preferred_element_type=jnp.float32)
    hidden = jnp.sin(preact)
    modulated = jnp.einsum("to,oc->ct", hidden, filter_out, precision=PRECISE)
    relative = column_pos.astype(jnp.float32) / length
    spread = jnp.sqrt(jnp.expm1(-2.0 * rates) / jnp.expm1(-2.0 * rates / length))
    envelope = jnp.exp(-rates[:, None] * relative[None, :]) / spread[:, None]
    kernel = (envelope * modulated).reshape(channels, devices, column_width)
    stacked = jnp.concatenate([columns[:channels], kernel, columns[channels:]], 0)
    cos_outer, sin_outer = angle_tables(devices, 2 * devices, 0, 0, 2 * devices)
    turned_real = jnp.einsum("ran,ak->rkn", stacked, cos_outer, precision=PRECISE)
    turned_imag = -jnp.einsum("ran,ak->rkn", stacked, sin_outer, precision=PRECISE)
    cos_turn, sin_turn = angle_tables(
        2 * devices, column_width, 0, device_index * column_width, modulus
    )
    turned_real, turned_imag = rotate(turned_real, turned_imag, cos_turn, sin_turn, -1.0)
    moved_real, moved_imag = (
        lax.all_to_all(turned_real, "seq", split_axis=1, concat_axis=2, tiled=True),
        lax.all_to_all(turned_imag, "seq", split_axis=1, concat_axis=2, tiled=True),
    )
    row_total = moved_real.shape[0]
    cos_first, sin_first = angle_tables(first_split, first_split, 0, 0, first_split)
    cos_second, sin_second = angle_tables(second_split, second_split, 0, 0, second_split)
    cos_mid, sin_mid = angle_tables(first_split, second_split, 0, 0, tokens_here)
    grid_real = moved_real.reshape(row_total, 2, first_split, second_split)
    grid_imag = moved_imag.reshape(row_total, 2, first_split, second_split)
    grid_real, grid_imag = dft_axis(
        grid_real, grid_imag, "rkab,ac->rkcb", cos_first, sin_first, -1.0
    )
    grid_real, grid_imag = rotate(grid_real, grid_imag, cos_mid, sin_mid, -1.0)
    spec_real, spec_imag = dft_axis(
        grid_real, grid_imag, "rkcb,bd->rkcd", cos_second, sin_second, -1.0
    )
    gated_real, gated_imag = (spec_real[:channels], spec_imag[:channels])
    kernel_real, kernel_imag = (
        spec_real[channels : 2 * channels],
        spec_imag[channels : 2 * channels],
    )
    grad_real, grad_imag = (spec_real[2 * channels :], spec_imag[2 * channels :])
    conv_real = gated_real * kernel_real - gated_imag * kernel_imag
    conv_imag = gated_real * kernel_imag + gated_imag * kernel_real
    back_real = grad_real * kernel_real + grad_imag * kernel_imag
    back_imag = grad_imag * kernel_real - grad_real * kernel_imag
    kgrad_real = grad_real * gated_real + grad_imag * gated_imag
    kgrad_imag = grad_imag * gated_real - grad_real * gated_imag
    cos_back, sin_back = angle_tables(2, tokens_here, 2 * device_index, 0, modulus)
    cos_last, sin_last = angle_tables(2 * devices, devices, 0, 0, 2 * devices)
    real_part = jnp.concatenate([conv_real, back_real, kgrad_real], 0)
    rows = real_part.shape[0]
    part_real, part_imag = dft_axis(
        real_part,
        jnp.concatenate([conv_imag, back_imag, kgrad_imag], 0),
        "rkcd,db->rkcb",
        cos_second,
        sin_second,
        1.0,
    )
    part_real, part_imag = rotate(part_real, part_imag, cos_mid, sin_mid, 1.0)
    part_real, part_imag = dft_axis(
        part_real, part_imag, "rkcb,ca->rkab", cos_first, sin_first, 1.0
    )
    part_real = part_real.reshape(rows, 2, tokens_here)
    part_imag = part_imag.reshape(rows, 2, tokens_here)
    part_real, part_imag = rotate(part_real, part_imag, cos_back[None], sin_back[None], 1.0)
    spread_real = lax.all_to_all(part_real, "seq", split_axis=2, concat_axis=1, tiled=True)
    spread_imag = lax.all_to_all(part_imag, "seq", split_axis=2, concat_axis=1, tiled=True)
    real_out = jnp.einsum("rkn,ka->ran", spread_real, cos_last, precision=PRECISE)
    real_out = (real_out - jnp.einsum("rkn,ka->ran", spread_imag, sin_last, precision=PRECISE)) * (
        1.0 / modulus
    )
    conv_cols = real_out[:channels]
    gated_cols = real_out[channels : 2 * channels]
    kernel_grad = real_out[2 * channels :]
    returned = lax.all_to_all(
        jnp.concatenate([conv_cols, gated_cols], 0), "seq", split_axis=1, concat_axis=2, tiled=True
    )
    returned = returned.reshape(2 * channels, tokens_here)
    conv_out = returned[:channels]
    grad_gated = returned[channels:]
    grad_mixed = jnp.stack(
        [cotangent_full * conv_out, grad_gated * value_part, grad_gated * key_part]
    )
    short_part = jnp.stack(
        [jnp.sum(grad_mixed * delayed(offset), axis=2) for offset in range(tap_count)], axis=2
    )
    weighted = envelope * kernel_grad.reshape(channels, devices * column_width)
    out_part = jnp.einsum("to,ct->oc", hidden, weighted, precision=PRECISE)
    grad_hidden = jnp.einsum("ct,oc->to", weighted, filter_out, precision=PRECISE)
    in_part = jnp.einsum("tf,to->fo", features, grad_hidden * jnp.cos(preact), precision=PRECISE)
    next_rim = shifted(grad_mixed[:, :, : tap_count - 1], "seq", -1)
    grad_extended = jnp.concatenate([grad_mixed, next_rim], 2)
    result = short_w[:, :, 0, None] * grad_extended[:, :, 0:tokens_here]
    for offset in range(1, tap_count):
        result = (
            result
            + short_w[:, :, offset, None] * grad_extended[:, :, offset : offset + tokens_here]
        )
    grad_proj = result.astype(jnp.bfloat16)
    short_total, out_total = lax.psum((short_part, out_part), "seq")
    in_total = lax.psum(in_part, ("seq", "ch"))
    return (grad_proj, short_total * norm_scale, out_total * norm_scale, in_total * norm_scale)


def solution(mesh):
    placed = (
        P(None, "ch", "seq"),
        P("ch", "seq"),
        P(None, "ch", None),
        P(),
        P(None, "ch"),
        P("ch"),
    )
    return jax.shard_map(
        shards,
        mesh=mesh,
        in_specs=placed,
        out_specs=(P(None, "ch", "seq"), P(None, "ch", None), P(None, "ch"), P()),
        check_vma=False,
    )
```

profile of v0, /device:TPU:8, one launch (start us, length us, event | category | flops | bytes accessed | tf_op | source)
XLA Modules:
  0.0 598.5 jit_solution(10087766709720511439)
XLA Ops:
  4.3 5.1 fusion.244
  12.4 3.8 reduce
  18.3 13.3 %all-to-all-start = ((f32[64,1,1024]{2,1,0:T(1,128)}), f32[64,1,1024]{2,1,0:T(1,128)}, u32[]{:S(2)}, u32[]{:S(2)}) async-start(f32[64,1,1024]{2,1,0:T(1,128)} %reshape.320), calls=%async_computation | async-start | bytes 524288 | tf_op jit(solution)/shard_map/all_to_all | solution.py:78
  37.6 5.8 all-to-all-done
  43.4 2.9 reduce.1
  53.9 2.9 add_bitcast_fusion.1
  59.4 6.3 %all-to-all-start.2 = ((f32[96,128,16]{0,2,1:T(8,128)}), f32[96,128,16]{0,2,1:T(8,128)}, u32[]{:S(2)}, u32[]{:S(2)}) async-start(f32[96,128,16]{0,2,1:T(8,128)} %copy.152), calls=%async_computation.2 | async-start | bytes 2097152 | tf_op jit(solution)/shard_map/all_to_all | solution.py:100
  68.2 25.5 %all-to-all-done.2 = f32[96,128,16]{0,2,1:T(8,128)} async-done(((f32[96,128,16]{0,2,1:T(8,128)}), f32[96,128,16]{0,2,1:T(8,128)}, u32[]{:S(2)}, u32[]{:S(2)}) %all-to-all-start.2) | async-done | bytes 786464 | tf_op jit(solution)/shard_map/all_to_all | solution.py:100
  93.7 7.2 %all-to-all-start.1 = ((f32[96,128,16]{0,2,1:T(8,128)}), f32[96,128,16]{0,2,1:T(8,128)}, u32[]{:S(2)}, u32[]{:S(2)}) async-start(f32[96,128,16]{0,2,1:T(8,128)} %copy.150), calls=%async_computation.1 | async-start | bytes 2097152 | tf_op jit(solution)/shard_map/all_to_all | solution.py:99
  101.4 3.8 fusion.14
  105.3 23.3 %all-to-all-done.1 = f32[96,128,16]{0,2,1:T(8,128)} async-done(((f32[96,128,16]{0,2,1:T(8,128)}), f32[96,128,16]{0,2,1:T(8,128)}, u32[]{:S(2)}, u32[]{:S(2)}) %all-to-all-start.1) | async-done | bytes 786464 | tf_op jit(solution)/shard_map/all_to_all | solution.py:99
  128.5 2.9 fusion.18
  131.5 2.9 fusion.7
  134.4 3.4 subtract_bitcast_fusion
  163.5 6.8 %all-to-all-start.3 = ((f32[96,2,1024]{0,1,2:T(2,128)}), f32[96,2,1024]{0,1,2:T(2,128)}, u32[]{:S(2)}, u32[]{:S(2)}) async-start(f32[96,2,1024]{0,1,2:T(2,128)} %copy.166), calls=%async_computation.3 | async-start | bytes 2097152 | tf_op jit(solution)/shard_map/all_to_all | solution.py:146
  170.4 3.0 copy.170
  173.4 25.0 %all-to-all-done.3 = f32[96,2,1024]{0,1,2:T(2,128)} async-done(((f32[96,2,1024]{0,1,2:T(2,128)}), f32[96,2,1024]{0,1,2:T(2,128)}, u32[]{:S(2)}, u32[]{:S(2)}) %all-to-all-start.3) | async-done | bytes 786464 | tf_op jit(solution)/shard_map/all_to_all | solution.py:146
  198.4 6.8 %all-to-all-start.4 = ((f32[96,2,1024]{0,1,2:T(2,128)}), f32[96,2,1024]{0,1,2:T(2,128)}, u32[]{:S(2)}, u32[]{:S(2)}) async-start(f32[96,2,1024]{0,1,2:T(2,128)} %copy.170), calls=%async_computation.4 | async-start | bytes 2097152 | tf_op jit(solution)/shard_map/all_to_all | solution.py:147
  208.5 24.7 %all-to-all-done.4 = f32[96,2,1024]{0,1,2:T(2,128)} async-done(((f32[96,2,1024]{0,1,2:T(2,128)}), f32[96,2,1024]{0,1,2:T(2,128)}, u32[]{:S(2)}, u32[]{:S(2)}) %all-to-all-start.4) | async-done | bytes 786464 | tf_op jit(solution)/shard_map/all_to_all | solution.py:147
  240.9 7.0 %all-to-all-start.5 = ((f32[64,1,1024]{2,1,0:T(1,128)}), f32[64,1,1024]{2,1,0:T(1,128)}, u32[]{:S(2)}, u32[]{:S(2)}) async-start(f32[64,1,1024]{2,1,0:T(1,128)} %reshape.322), calls=%async_computation.5 | async-start | bytes 524288 | tf_op jit(solution)/shard_map/all_to_all | solution.py:155
  254.1 3.0 fusion.43
  257.1 75.9 %psum.23 = f32[32,64]{1,0:T(8,128)S(1)} all-reduce(f32[32,64]{1,0:T(8,128)S(1)} %fusion.43), channel_id=1, replica_groups=mesh['seq'=64,'ch'=4] {'seq','ch'}, use_global_device_ids=true, to_apply=%region_5.6 | all-reduce | flops 2048 | bytes 16384 | tf_op jit(solution)/shard_map/psum | solution.py:181
  334.4 2.9 reduce.2
  346.4 250.5 %all-reduce = (f32[3,32,3]{1,0,2:T(4,128)S(1)}, f32[64,32]{0,1:T(8,128)S(1)}) all-reduce(f32[3,32,3]{1,0,2:T(4,128)S(1)} %pad_maximum_fusion.7, f32[64,32]{0,1:T(8,128)S(1)} %fusion.238), channel_id=1, replica_groups=mesh['seq'=64,'ch'=4] {'seq'}, use_global_device_ids=true, to_apply=%region_3.4 | all-reduce | flops 2336 | bytes 18688 | tf_op jit(solution)/shard_map/psum | solution.py:180
  (118 shorter events, 82.0 us)
Async XLA Ops:
  0.6 3.7 copy-start
  0.6 8.8 %copy-start.6 = (bf16[32,1024]{1,0:T(8,128)(2,1)S(1)}, bf16[32,1024]{1,0:T(8,128)(2,1)}, u32[]{:S(2)}) copy-start(bf16[32,1024]{1,0:T(8,128)(2,1)} %param.7) | copy-start | bytes 196612
  1.5 8.1 %collective-permute-start = (bf16[3,32,2]{2,1,0:T(8,128)(2,1)S(1)}, bf16[3,32,2]{2,1,0:T(8,128)(2,1)S(1)}, u32[]{:S(2)}, u32[]{:S(2)}) collective-permute-start(bf16[3,32,2]{2,1,0:T(8,128)(2,1)S(1)} %slice.96), channel_id=1, source_target_pairs={{0,4},{4,8},{8,12},{12,16},{16,20},{20,24},{24,28},{28,32},{32,36}... | collective-permute-start | bytes 1160 | tf_op jit(solution)/shard_map/ppermute | solution.py:13
  3.3 6.3 %copy-start.10 = (s32[32]{0:T(128)}, s32[32]{0:T(128)S(1)}, u32[]{:S(2)}) copy-start(s32[32]{0:T(128)S(1)} %get-tuple-element.66) | copy-start | bytes 388
  3.3 6.3 %copy-start.12 = (pred[32]{0:T(512)(128)(4,1)}, pred[32]{0:T(512)(128)(4,1)S(1)}, u32[]{:S(2)}) copy-start(pred[32]{0:T(512)(128)(4,1)S(1)} %fusion.143) | copy-start | bytes 100
  4.3 5.3 copy-start.5
  11.9 19.7 %copy-start.9 = (f32[32]{0:T(128)S(1)}, f32[32]{0:T(128)}, u32[]{:S(2)}) copy-start(f32[32]{0:T(128)} %param.11) | copy-start | bytes 388
  11.9 19.7 %copy-start.7 = (f32[64,32]{0,1:T(8,128)S(1)}, f32[64,32]{0,1:T(8,128)}, u32[]{:S(2)}) copy-start(f32[64,32]{0,1:T(8,128)} %param.10) | copy-start | bytes 24580
  18.3 25.2 %all-to-all-start = ((f32[64,1,1024]{2,1,0:T(1,128)}), f32[64,1,1024]{2,1,0:T(1,128)}, u32[]{:S(2)}, u32[]{:S(2)}) async-start(f32[64,1,1024]{2,1,0:T(1,128)} %reshape.320), calls=%async_computation | async-start | bytes 524288 | tf_op jit(solution)/shard_map/all_to_all | solution.py:78
  51.1 1.0 copy-start.2
  59.4 34.3 %all-to-all-start.2 = ((f32[96,128,16]{0,2,1:T(8,128)}), f32[96,128,16]{0,2,1:T(8,128)}, u32[]{:S(2)}, u32[]{:S(2)}) async-start(f32[96,128,16]{0,2,1:T(8,128)} %copy.152), calls=%async_computation.2 | async-start | bytes 2097152 | tf_op jit(solution)/shard_map/all_to_all | solution.py:100
  93.7 34.9 %all-to-all-start.1 = ((f32[96,128,16]{0,2,1:T(8,128)}), f32[96,128,16]{0,2,1:T(8,128)}, u32[]{:S(2)}, u32[]{:S(2)}) async-start(f32[96,128,16]{0,2,1:T(8,128)} %copy.150), calls=%async_computation.1 | async-start | bytes 2097152 | tf_op jit(solution)/shard_map/all_to_all | solution.py:99
  128.5 3.0 copy-start.3
  163.5 34.9 %all-to-all-start.3 = ((f32[96,2,1024]{0,1,2:T(2,128)}), f32[96,2,1024]{0,1,2:T(2,128)}, u32[]{:S(2)}, u32[]{:S(2)}) async-start(f32[96,2,1024]{0,1,2:T(2,128)} %copy.166), calls=%async_computation.3 | async-start | bytes 2097152 | tf_op jit(solution)/shard_map/all_to_all | solution.py:146
  198.4 34.9 %all-to-all-start.4 = ((f32[96,2,1024]{0,1,2:T(2,128)}), f32[96,2,1024]{0,1,2:T(2,128)}, u32[]{:S(2)}, u32[]{:S(2)}) async-start(f32[96,2,1024]{0,1,2:T(2,128)} %copy.170), calls=%async_computation.4 | async-start | bytes 2097152 | tf_op jit(solution)/shard_map/all_to_all | solution.py:147
  234.5 1.0 copy-start.4
  238.8 13.1 %copy-start.8 = (f32[64,32]{0,1:T(8,128)S(1)}, f32[64,32]{0,1:T(8,128)}, u32[]{:S(2)}) copy-start(f32[64,32]{0,1:T(8,128)} %param.10) | copy-start | bytes 24580
  240.9 13.2 %copy-start.11 = (s32[32]{0:T(128)S(1)}, s32[32]{0:T(128)}, u32[]{:S(2)}) copy-start(s32[32]{0:T(128)} %copy-done.10) | copy-start | bytes 388
  240.9 13.2 %copy-start.13 = (pred[32]{0:T(512)(128)(4,1)S(1)}, pred[32]{0:T(512)(128)(4,1)}, u32[]{:S(2)}) copy-start(pred[32]{0:T(512)(128)(4,1)} %copy-done.12) | copy-start | bytes 100
  240.9 93.6 %all-to-all-start.5 = ((f32[64,1,1024]{2,1,0:T(1,128)}), f32[64,1,1024]{2,1,0:T(1,128)}, u32[]{:S(2)}, u32[]{:S(2)}) async-start(f32[64,1,1024]{2,1,0:T(1,128)} %reshape.322), calls=%async_computation.5 | async-start | bytes 524288 | tf_op jit(solution)/shard_map/all_to_all | solution.py:155
  341.0 3.1 collective-permute-start.1
  344.1 253.9 %copy-start.1 = (f32[32,64]{1,0:T(8,128)S(1)}, f32[32,64]{1,0:T(8,128)}, u32[]{:S(2)}) copy-start(f32[32,64]{1,0:T(8,128)} %param.9) | copy-start | bytes 24580
where the time goes:
time: 605 us; the launch traced here: 599 us
  blocking collectives  326 us (54%)
  waiting for transfers between devices  106 us (18%)
  matrix products  52.9 us (9%)
  starting transfers between devices  50.4 us (8%)
  local copies, waits for them, and re-layouts  42.8 us (7%)
  other arithmetic  18.9 us (3%)
    psum x1, blocking collectives, shards(): short_total, out_total = lax.psum((short_part, out_part), 'seq')  250 us
    psum x1, blocking collectives, shards(): in_total = lax.psum(in_part, ('seq', 'ch'))  75.9 us
    all_to_all x1, waiting for transfers between devices, shards(): lax.all_to_all(turned_imag, 'seq', split_axis=1, concat_axis=2, tiled=True)  25.5 us
    all_to_all x1, waiting for transfers between devices, shards(): lax.all_to_all(part_real, 'seq', split_axis=2, concat_axis=1, tiled=True)  25 us
    all_to_all x1, waiting for transfers between devices, shards(): lax.all_to_all(part_imag, 'seq', split_axis=2, concat_axis=1, tiled=True)  24.7 us
    all_to_all x1, waiting for transfers between devices, shards(): lax.all_to_all(turned_real, 'seq', split_axis=1, concat_axis=2, tiled=True)  23.3 us
    all_to_all x1, starting transfers between devices, shards(): lax.all_to_all(both_signals, 'seq', split_axis=2, concat_axis=1, tiled=True)  13.3 us
    unnamed x38, local copies, waits for them, and re-layouts  12.3 us
  transfers between devices with their start and end apart: 8, of which 6 were waited for; matrix products, arithmetic and copies ran while one was open for 6% of the time, Pallas kernels for 0%

commit v1 on v0

--- a/solution.py
+++ b/solution.py
@@ -178,7 +178,7 @@
         )
     grad_proj = result.astype(jnp.bfloat16)
     short_total, out_total = lax.psum((short_part, out_part), "seq")
-    in_total = lax.psum(in_part, ("seq", "ch"))
+    in_total = lax.psum(lax.psum(in_part, "seq"), "ch")
     return (grad_proj, short_total * norm_scale, out_total * norm_scale, in_total * norm_scale)
 
 

time: 605 us -> 546 us (0.902)
  blocking collectives: 326 us -> 264 us
    psum x1, blocking collectives: 75.9 us -> 14.1 us  [shards(): in_total = lax.psum(lax.psum(in_part, 'seq'), 'ch')]
    unnamed x38 -> x42, local copies, waits for them, and re-layouts: 12.3 us -> 13.1 us
  transfers between devices with their start and end apart: 8 -> 8, of which waited for: 6 -> 6; matrix products, arithmetic and copies ran while one was open for 6% -> 7% of each run, Pallas kernels for 0% -> 0%
where the time goes in v1:
time: 546 us; the launch traced here: 538 us
  blocking collectives  264 us (48%)
  waiting for transfers between devices  108 us (20%)
  matrix products  53.6 us (10%)
  starting transfers between devices  50.3 us (9%)
  local copies, waits for them, and re-layouts  42.7 us (8%)
  other arithmetic  18.8 us (3%)
    psum x1, blocking collectives, shards(): short_total, out_total = lax.psum((short_part, out_part), 'seq')  249 us
    all_to_all x1, waiting for transfers between devices, shards(): lax.all_to_all(turned_imag, 'seq', split_axis=1, concat_axis=2, tiled=True)  25.5 us
    all_to_all x1, waiting for transfers between devices, shards(): lax.all_to_all(part_real, 'seq', split_axis=2, concat_axis=1, tiled=True)  25 us
    all_to_all x1, waiting for transfers between devices, shards(): lax.all_to_all(part_imag, 'seq', split_axis=2, concat_axis=1, tiled=True)  24.7 us
    all_to_all x1, waiting for transfers between devices, shards(): lax.all_to_all(turned_real, 'seq', split_axis=1, concat_axis=2, tiled=True)  23.3 us
    psum x1, blocking collectives, shards(): in_total = lax.psum(lax.psum(in_part, 'seq'), 'ch')  14.1 us
    all_to_all x1, starting transfers between devices, shards(): lax.all_to_all(both_signals, 'seq', split_axis=2, concat_axis=1, tiled=True)  13.3 us
    unnamed x42, local copies, waits for them, and re-layouts  13.1 us
  transfers between devices with their start and end apart: 8, of which 6 were waited for; matrix products, arithmetic and copies ran while one was open for 7% of the time, Pallas kernels for 0%

profile of v1, /device:TPU:8, one launch (start us, length us, event | category | flops | bytes accessed | tf_op | source)
XLA Modules:
  0.0 538.4 jit_solution(1813360750721617488)
XLA Ops:
  4.3 5.1 fusion.244
  12.4 3.8 reduce
  18.3 13.3 %all-to-all-start = ((f32[64,1,1024]{2,1,0:T(1,128)}), f32[64,1,1024]{2,1,0:T(1,128)}, u32[]{:S(2)}, u32[]{:S(2)}) async-start(f32[64,1,1024]{2,1,0:T(1,128)} %reshape.320), calls=%async_computation | async-start | bytes 524288 | tf_op jit(solution)/shard_map/all_to_all | solution.py:78
  37.6 5.9 %all-to-all-done = f32[64,1,1024]{2,1,0:T(1,128)} async-done(((f32[64,1,1024]{2,1,0:T(1,128)}), f32[64,1,1024]{2,1,0:T(1,128)}, u32[]{:S(2)}, u32[]{:S(2)}) %all-to-all-start) | async-done | bytes 262176 | tf_op jit(solution)/shard_map/all_to_all | solution.py:78
  43.4 2.9 reduce.1
  59.4 6.3 %all-to-all-start.2 = ((f32[96,128,16]{0,2,1:T(8,128)}), f32[96,128,16]{0,2,1:T(8,128)}, u32[]{:S(2)}, u32[]{:S(2)}) async-start(f32[96,128,16]{0,2,1:T(8,128)} %copy.152), calls=%async_computation.2 | async-start | bytes 2097152 | tf_op jit(solution)/shard_map/all_to_all | solution.py:100
  68.1 25.5 %all-to-all-done.2 = f32[96,128,16]{0,2,1:T(8,128)} async-done(((f32[96,128,16]{0,2,1:T(8,128)}), f32[96,128,16]{0,2,1:T(8,128)}, u32[]{:S(2)}, u32[]{:S(2)}) %all-to-all-start.2) | async-done | bytes 786464 | tf_op jit(solution)/shard_map/all_to_all | solution.py:100
  93.7 7.2 %all-to-all-start.1 = ((f32[96,128,16]{0,2,1:T(8,128)}), f32[96,128,16]{0,2,1:T(8,128)}, u32[]{:S(2)}, u32[]{:S(2)}) async-start(f32[96,128,16]{0,2,1:T(8,128)} %copy.150), calls=%async_computation.1 | async-start | bytes 2097152 | tf_op jit(solution)/shard_map/all_to_all | solution.py:99
  101.4 3.8 fusion.14
  105.3 23.3 %all-to-all-done.1 = f32[96,128,16]{0,2,1:T(8,128)} async-done(((f32[96,128,16]{0,2,1:T(8,128)}), f32[96,128,16]{0,2,1:T(8,128)}, u32[]{:S(2)}, u32[]{:S(2)}) %all-to-all-start.1) | async-done | bytes 786464 | tf_op jit(solution)/shard_map/all_to_all | solution.py:99
  128.5 2.9 fusion.18
  134.4 3.4 subtract_bitcast_fusion
  163.5 6.8 %all-to-all-start.3 = ((f32[96,2,1024]{0,1,2:T(2,128)}), f32[96,2,1024]{0,1,2:T(2,128)}, u32[]{:S(2)}, u32[]{:S(2)}) async-start(f32[96,2,1024]{0,1,2:T(2,128)} %copy.166), calls=%async_computation.3 | async-start | bytes 2097152 | tf_op jit(solution)/shard_map/all_to_all | solution.py:146
  170.3 3.1 copy.170
  173.4 25.0 %all-to-all-done.3 = f32[96,2,1024]{0,1,2:T(2,128)} async-done(((f32[96,2,1024]{0,1,2:T(2,128)}), f32[96,2,1024]{0,1,2:T(2,128)}, u32[]{:S(2)}, u32[]{:S(2)}) %all-to-all-start.3) | async-done | bytes 786464 | tf_op jit(solution)/shard_map/all_to_all | solution.py:146
  198.4 6.8 %all-to-all-start.4 = ((f32[96,2,1024]{0,1,2:T(2,128)}), f32[96,2,1024]{0,1,2:T(2,128)}, u32[]{:S(2)}, u32[]{:S(2)}) async-start(f32[96,2,1024]{0,1,2:T(2,128)} %copy.170), calls=%async_computation.4 | async-start | bytes 2097152 | tf_op jit(solution)/shard_map/all_to_all | solution.py:147
  208.5 24.7 %all-to-all-done.4 = f32[96,2,1024]{0,1,2:T(2,128)} async-done(((f32[96,2,1024]{0,1,2:T(2,128)}), f32[96,2,1024]{0,1,2:T(2,128)}, u32[]{:S(2)}, u32[]{:S(2)}) %all-to-all-start.4) | async-done | bytes 786464 | tf_op jit(solution)/shard_map/all_to_all | solution.py:147
  240.6 6.8 %all-to-all-start.5 = ((f32[64,1,1024]{2,1,0:T(1,128)}), f32[64,1,1024]{2,1,0:T(1,128)}, u32[]{:S(2)}, u32[]{:S(2)}) async-start(f32[64,1,1024]{2,1,0:T(1,128)} %reshape.322), calls=%async_computation.5 | async-start | bytes 524288 | tf_op jit(solution)/shard_map/all_to_all | solution.py:155
  253.1 2.9 convolution_multiply_fusion.4
  256.0 3.3 all-to-all-done.5
  259.3 2.9 reduce.2
  267.1 3.0 fusion.43
  272.5 249.5 %all-reduce = (f32[3,32,3]{1,0,2:T(4,128)S(1)}, f32[64,32]{0,1:T(8,128)S(1)}, f32[32,64]{1,0:T(8,128)S(1)}) all-reduce(f32[3,32,3]{1,0,2:T(4,128)S(1)} %pad_maximum_fusion.7, f32[64,32]{0,1:T(8,128)S(1)} %fusion.238, f32[32,64]{1,0:T(8,128)S(1)} %fusion.43), channel_id=1, replica_groups=mesh['seq'=64,'ch'=4] {'seq'}, use_global_device_ids=true, to_apply=%region_3.4 | all-reduce | flops 4384 | bytes 35072 | tf_op jit(solution)/shard_map/psum | solution.py:180
  523.2 14.1 %psum.31 = f32[32,64]{1,0:T(8,128)S(1)} all-reduce(f32[32,64]{1,0:T(8,128)S(1)} %get-tuple-element.29), channel_id=1, replica_groups=mesh['seq'=64,'ch'=4] {'ch'}, use_global_device_ids=true, to_apply=%region_6.7 | all-reduce | flops 2048 | bytes 16384 | tf_op jit(solution)/shard_map/psum | solution.py:181
  (122 shorter events, 84.3 us)
Async XLA Ops:
  0.6 3.7 copy-start
  0.6 8.8 %copy-start.7 = (bf16[32,1024]{1,0:T(8,128)(2,1)S(1)}, bf16[32,1024]{1,0:T(8,128)(2,1)}, u32[]{:S(2)}) copy-start(bf16[32,1024]{1,0:T(8,128)(2,1)} %param.7) | copy-start | bytes 196612
  1.5 8.1 %collective-permute-start = (bf16[3,32,2]{2,1,0:T(8,128)(2,1)S(1)}, bf16[3,32,2]{2,1,0:T(8,128)(2,1)S(1)}, u32[]{:S(2)}, u32[]{:S(2)}) collective-permute-start(bf16[3,32,2]{2,1,0:T(8,128)(2,1)S(1)} %slice.96), channel_id=1, source_target_pairs={{0,4},{4,8},{8,12},{12,16},{16,20},{20,24},{24,28},{28,32},{32,36}... | collective-permute-start | bytes 1160 | tf_op jit(solution)/shard_map/ppermute | solution.py:13
  3.3 6.4 %copy-start.12 = (s32[32]{0:T(128)}, s32[32]{0:T(128)S(1)}, u32[]{:S(2)}) copy-start(s32[32]{0:T(128)S(1)} %get-tuple-element.67) | copy-start | bytes 388
  3.3 6.3 %copy-start.14 = (pred[32]{0:T(512)(128)(4,1)}, pred[32]{0:T(512)(128)(4,1)S(1)}, u32[]{:S(2)}) copy-start(pred[32]{0:T(512)(128)(4,1)S(1)} %fusion.143) | copy-start | bytes 100
  4.3 5.3 copy-start.6
  11.9 19.7 %copy-start.10 = (f32[32]{0:T(128)S(1)}, f32[32]{0:T(128)}, u32[]{:S(2)}) copy-start(f32[32]{0:T(128)} %param.11) | copy-start | bytes 388
  11.9 19.7 %copy-start.8 = (f32[64,32]{0,1:T(8,128)S(1)}, f32[64,32]{0,1:T(8,128)}, u32[]{:S(2)}) copy-start(f32[64,32]{0,1:T(8,128)} %param.10) | copy-start | bytes 24580
  18.3 25.2 %all-to-all-start = ((f32[64,1,1024]{2,1,0:T(1,128)}), f32[64,1,1024]{2,1,0:T(1,128)}, u32[]{:S(2)}, u32[]{:S(2)}) async-start(f32[64,1,1024]{2,1,0:T(1,128)} %reshape.320), calls=%async_computation | async-start | bytes 524288 | tf_op jit(solution)/shard_map/all_to_all | solution.py:78
  51.2 1.0 copy-start.2
  59.4 34.3 %all-to-all-start.2 = ((f32[96,128,16]{0,2,1:T(8,128)}), f32[96,128,16]{0,2,1:T(8,128)}, u32[]{:S(2)}, u32[]{:S(2)}) async-start(f32[96,128,16]{0,2,1:T(8,128)} %copy.152), calls=%async_computation.2 | async-start | bytes 2097152 | tf_op jit(solution)/shard_map/all_to_all | solution.py:100
  93.7 34.9 %all-to-all-start.1 = ((f32[96,128,16]{0,2,1:T(8,128)}), f32[96,128,16]{0,2,1:T(8,128)}, u32[]{:S(2)}, u32[]{:S(2)}) async-start(f32[96,128,16]{0,2,1:T(8,128)} %copy.150), calls=%async_computation.1 | async-start | bytes 2097152 | tf_op jit(solution)/shard_map/all_to_all | solution.py:99
  128.5 3.0 copy-start.4
  163.5 34.9 %all-to-all-start.3 = ((f32[96,2,1024]{0,1,2:T(2,128)}), f32[96,2,1024]{0,1,2:T(2,128)}, u32[]{:S(2)}, u32[]{:S(2)}) async-start(f32[96,2,1024]{0,1,2:T(2,128)} %copy.166), calls=%async_computation.3 | async-start | bytes 2097152 | tf_op jit(solution)/shard_map/all_to_all | solution.py:146
  198.4 34.9 %all-to-all-start.4 = ((f32[96,2,1024]{0,1,2:T(2,128)}), f32[96,2,1024]{0,1,2:T(2,128)}, u32[]{:S(2)}, u32[]{:S(2)}) async-start(f32[96,2,1024]{0,1,2:T(2,128)} %copy.170), calls=%async_computation.4 | async-start | bytes 2097152 | tf_op jit(solution)/shard_map/all_to_all | solution.py:147
  234.5 1.0 copy-start.5
  236.6 0.8 copy-start.3
  240.6 18.7 %all-to-all-start.5 = ((f32[64,1,1024]{2,1,0:T(1,128)}), f32[64,1,1024]{2,1,0:T(1,128)}, u32[]{:S(2)}, u32[]{:S(2)}) async-start(f32[64,1,1024]{2,1,0:T(1,128)} %reshape.322), calls=%async_computation.5 | async-start | bytes 524288 | tf_op jit(solution)/shard_map/all_to_all | solution.py:155
  247.5 5.6 %copy-start.9 = (f32[64,32]{0,1:T(8,128)S(1)}, f32[64,32]{0,1:T(8,128)}, u32[]{:S(2)}) copy-start(f32[64,32]{0,1:T(8,128)} %param.10) | copy-start | bytes 24580
  265.7 1.5 copy-start.11
  265.7 1.5 copy-start.13
  265.7 1.5 copy-start.15
  265.8 4.4 collective-permute-start.1
  270.3 267.7 %copy-start.1 = (f32[32,64]{1,0:T(8,128)S(1)}, f32[32,64]{1,0:T(8,128)}, u32[]{:S(2)}) copy-start(f32[32,64]{1,0:T(8,128)} %param.9) | copy-start | bytes 24580
